TPU v7x, 128 devices: a whole 4x4x4 slice. The times are simulated.
128 devices in a mesh: gene: 8 (over y, x_lo), bin: 16 (over z, x_hi, core).
Axes of the slice: x: 4 (x_hi: 2, x_lo: 2; x = x_hi * 2 + x_lo), y: 4, z: 4, core: 2. Of those that a mesh axis runs over, the one named last changes fastest.
Arguments:
- counts: bfloat16 [49152, 18432], P('bin', 'gene'), may hold values from 2 to 80
- factors: float32 [49152, 256], P('bin'), may hold values from 0.01 to 1
- loadings: float32 [256, 18432], P(None, 'gene'), may hold values from 0.01 to 1
- position: int32 [49152], P('bin'), may hold values from 0 to 49151, as said below
- edge_codes: int32 [192, 256], P('bin'), may hold values from 1 to 15
Outputs:
- factors_new: float32 [49152, 256], P('bin')
- loadings_new: float32 [256, 18432], P(None, 'gene')
Inputs may be any that keep to these rules, and one draw needn't show every extreme that they name: Each grid position is named by exactly one barcode. The barcodes of one index s of bin (rows s * 3072 on) fall in 16 aligned groups of 192; group t holds positions in grid rows t * 12 to (t + 1) * 12 - 1, 192 from every such index.
All inputs are finite; a program needn't handle non-finite values.
Results may differ from a plain program's by a relative error of at most 0.0003.
Values sent between devices are 32-bit elements; how exact they have to be, the bound alone decides.
A program may use at most 128 MiB of HBM per device.

v0:
```python
import jax
import jax.numpy as jnp
from jax import lax
from jax.sharding import PartitionSpec as P

K = 256
G = 18432


def passed_along(block, axis, distance):
    devices = range(lax.axis_size(axis))
    route = [(i - distance, i) for i in devices if i - distance in devices]
    return lax.ppermute(block, axis, route)


def neighbour_sum(values, from_above, from_below):
    upper = jnp.concatenate([from_above[None], values[:-1]], 0)
    lower = jnp.concatenate([values[1:], from_below[None]], 0)
    beside = jnp.pad(values[:, 1:], ((0, 0), (0, 1), (0, 0))) + jnp.pad(
        values[:, :-1], ((0, 0), (1, 0), (0, 0))
    )
    return beside + 0.5 * (lower + upper)


def neighbour_first(values, from_above, from_below):
    upper = jnp.concatenate([from_above[:, None], values[:, :-1]], 1)
    lower = jnp.concatenate([values[:, 1:], from_below[:, None]], 1)
    beside = jnp.pad(values[:, :, 1:], ((0, 0), (0, 0), (0, 1))) + jnp.pad(
        values[:, :, :-1], ((0, 0), (0, 0), (1, 0))
    )
    return beside + 0.5 * (lower + upper)


def split_three(values):
    high = lax.reduce_precision(values, exponent_bits=8, mantissa_bits=7)
    rest = values - high
    mid = lax.reduce_precision(rest, exponent_bits=8, mantissa_bits=7)
    low = rest - mid
    return jnp.concatenate([high, mid, low], 1).astype(jnp.bfloat16)


def join_three(parts, width):
    return parts[:, :width] + parts[:, width : 2 * width] + parts[:, 2 * width :]


def stencil_term(own, position, edge_codes):
    bin_count = lax.axis_size("bin")
    row_count, width = own.shape
    group_size = row_count // bin_count
    grid_rows, grid_cols = edge_codes.shape
    payload = jnp.concatenate([own, position.astype(jnp.float32)[:, None]], 1)
    got = lax.all_to_all(
        payload.reshape(bin_count, group_size * (width + 1)), "bin", 0, 0, tiled=True
    ).reshape(row_count, width + 1)
    tile_slot = got[:, width].astype(jnp.int32) - lax.axis_index("bin") * row_count
    cells = lax.broadcasted_iota(jnp.int32, (row_count, row_count), 1)
    onehot = (tile_slot[:, None] == cells).astype(jnp.bfloat16)
    placed = lax.dot_general(
        onehot,
        split_three(got[:, :width]),
        (((0,), (0,)), ((), ())),
        preferred_element_type=jnp.float32,
    )
    tile_rows = join_three(placed, width)
    cell_scale = edge_codes.astype(jnp.float32) / 8.0
    weighted = cell_scale[:, :, None] * tile_rows.reshape(grid_rows, grid_cols, width)
    rim_last, rim_first = (weighted[-1], weighted[0])
    upper_rows, upper_scale = passed_along((rim_last, cell_scale[-1]), "bin", 1)
    lower_rows, lower_scale = passed_along((rim_first, cell_scale[0]), "bin", -1)
    degree_grid = (
        cell_scale * neighbour_first(cell_scale[None], upper_scale[None], lower_scale[None])[0]
    )
    smooth_grid = cell_scale[:, :, None] * neighbour_sum(weighted, upper_rows, lower_rows)
    back = jnp.concatenate(
        [smooth_grid.reshape(row_count, width), degree_grid.reshape(row_count, 1)], 1
    )
    back_rows = join_three(
        jnp.dot(onehot, split_three(back), preferred_element_type=jnp.float32), width + 1
    )
    ret = lax.all_to_all(
        back_rows.reshape(bin_count, group_size * (width + 1)), "bin", 0, 0, tiled=True
    ).reshape(row_count, width + 1)
    return (ret[:, :width], ret[:, width])


def on_device(counts, factors, loadings, position, edge_codes):
    bin_count = lax.axis_size("bin")
    gene_count = lax.axis_size("gene")
    row_count, width_all = factors.shape
    group_size = row_count // bin_count
    width = width_all // gene_count
    k_rows = width_all // bin_count
    gene_at = lax.axis_index("gene")
    bin_at = lax.axis_index("bin")
    load_bf = loadings.astype(jnp.bfloat16)
    right_dims = (((1,), (1,)), ((), ()))
    numer_part = lax.dot_general(counts, load_bf, right_dims, preferred_element_type=jnp.float32)
    gram_part = lax.dot_general(load_bf, load_bf, right_dims, preferred_element_type=jnp.float32)
    both = lax.psum_scatter(
        jnp.concatenate([numer_part, gram_part], 0), "gene", scatter_dimension=1, tiled=True
    )
    numer, load_gram = (both[:row_count], both[row_count:])
    own = lax.dynamic_slice_in_dim(factors, gene_at * width, width, 1)
    smooth, degree = stencil_term(own, position, edge_codes)
    penalty = float(G * K) / 64.0
    denom = (
        jnp.dot(factors, load_gram, precision=lax.Precision.HIGHEST)
        + penalty * degree[:, None] * own
    )
    new_own = own * (numer + penalty * smooth) / denom
    factors_new = lax.all_gather(new_own, "gene", axis=1, tiled=True)
    fac_bf = factors_new.astype(jnp.bfloat16)
    left_dims = (((0,), (0,)), ((), ()))
    cross_part = lax.dot_general(fac_bf, counts, left_dims, preferred_element_type=jnp.float32)
    fgram_part = lax.dot_general(fac_bf, fac_bf, left_dims, preferred_element_type=jnp.float32)
    both_bin = lax.psum_scatter(
        jnp.concatenate([cross_part, fgram_part], 1), "bin", scatter_dimension=0, tiled=True
    )
    cross, fac_gram = (both_bin[:, : cross_part.shape[1]], both_bin[:, cross_part.shape[1] :])
    own_load = lax.dynamic_slice_in_dim(loadings, bin_at * k_rows, k_rows, 0)
    new_load = own_load * cross / jnp.dot(fac_gram, loadings, precision=lax.Precision.HIGHEST)
    loadings_new = lax.all_gather(new_load, "bin", axis=0, tiled=True)
    return (factors_new, loadings_new)


def solution(mesh):
    placed = (P("bin", "gene"), P("bin", None), P(None, "gene"), P("bin"), P("bin", None))
    return jax.shard_map(
        on_device,
        mesh=mesh,
        in_specs=placed,
        out_specs=(P("bin", None), P(None, "gene")),
        check_vma=False,
    )
```

profile of v0, /device:TPU:1, one launch (start us, length us, event | category | flops | bytes accessed | tf_op | source)
XLA Modules:
  0.0 368.8 jit_solution(11523954443179676951)
XLA Ops:
  7.2 1.9 copy-done
  9.1 1.6 constant_dynamic-slice_fusion
  10.7 1.8 copy.43
  12.5 0.8 pad_maximum_fusion.2
  13.4 2.7 copy.30
  16.0 3.8 %all_to_all.16 = f32[16,1,6336]{2,1,0:T(1,128)} reshape(f32[3072,33]{1,0:T(8,128)} %copy.30) | data formatting | bytes 811008 | tf_op jit(solution)/shard_map/all_to_all | solution.py:52
  19.9 9.3 %all-to-all-start = ((f32[16,1,6336]{2,1,0:T(1,128)}), f32[16,1,6336]{2,1,0:T(1,128)}, u32[]{:S(2)}, u32[]{:S(2)}) async-start(f32[16,1,6336]{2,1,0:T(1,128)} %all_to_all.16), calls=%async_computation | async-start | bytes 819200 | tf_op jit(solution)/shard_map/all_to_all | solution.py:52
  29.2 0.9 fusion.42
  30.7 2.0 collective-permute-start.2
  32.7 5.0 %collective-permute-start.3 = (f32[256]{0:T(256)}, f32[256]{0:T(256)}, u32[]{:S(2)}, u32[]{:S(2)}) collective-permute-start(f32[256]{0:T(256)} %bitcast.6), channel_id=1, source_target_pairs={{0,1},{1,2},{2,3},{3,4},{4,5},{5,6},{6,7},{7,8},{8,9},{9,10},{10,1... | collective-permute-start | bytes 3080 | tf_op jit(solution)/shard_map/ppermute | solution.py:13
  37.8 2.9 fusion.23
  40.7 7.2 %fusion.25 = f32[3072,256]{1,0:T(8,128)S(1)} fusion(bf16[3072,2304]{1,0:T(8,128)(2,1)} %param.5, f32[256,2304]{1,0:T(8,128)S(1)} %copy-done.2), kind=kOutput, calls=%fused_computation.36 | convolution fusion | flops 3624468480 | bytes 19660800 | tf_op jit(solution)/shard_map/dot_general | solution.py:97
  47.9 2.0 pad_maximum_fusion
  49.9 5.0 %copy.41 = f32[3328,256]{0,1:T(8,128)} copy(f32[3328,256]{1,0:T(8,128)} %pad_maximum_fusion) | data formatting | bytes 6815744
  56.8 0.9 fusion.39
  58.2 2.7 reduce
  61.0 4.0 %reshape.94 = f32[3072,33]{1,0:T(8,128)} reshape(f32[16,6336]{1,0:T(8,128)} %reduce) | data formatting | bytes 811008 | tf_op jit(solution)/shard_map/reshape | solution.py:54
  64.9 2.9 copy.44
  67.8 2.3 fusion.8
  70.1 1.1 reduce-precision_convert_fusion.3
  71.2 7.5 %fusion.1 = f32[3072,96]{0,1:T(8,128)S(1)} fusion(s32[3072]{0:T(1024)S(1)} %fusion.8, bf16[3072,32]{0,1:T(8,128)(2,1)S(1)} %get-tuple-element.16, bf16[3072,32]{0,1:T(8,128)(2,1)S(1)} %get-tuple-element.17, bf16[3072,32]{0,1:T(8,128)(2,1)S(1)} %get-tuple-element.15), kind=kOutput, calls=%fused_computation.2 | convolution fusion | flops 1823145984 | bytes 1781760 | tf_op jit(solution)/shard_map/dot_general | solution.py:58
  78.8 0.8 slice_add_fusion.2
  79.6 1.9 reshape.95
  81.5 1.1 broadcast_multiply_fusion
  82.6 1.9 collective-permute-start
  84.6 5.3 %collective-permute-start.1 = (f32[256,32]{0,1:T(8,128)S(1)}, f32[256,32]{0,1:T(8,128)S(1)}, u32[]{:S(2)}, u32[]{:S(2)}) collective-permute-start(f32[256,32]{0,1:T(8,128)S(1)} %bitcast.56), channel_id=1, source_target_pairs={{0,1},{1,2},{2,3},{3,4},{4,5},{5,6},{6,7},{7,8},{8,9},{9,10},{10,1... | collective-permute-start | bytes 98312 | tf_op jit(solution)/shard_map/ppermute | solution.py:13
  90.3 1.2 collective-permute-done.1
  92.0 0.8 constant_dynamic-update-slice_fusion
  92.8 1.6 dynamic-update-slice.1
  94.4 1.1 reduce-precision_convert_fusion.1
  95.5 8.0 %fusion = f32[3072,99]{0,1:T(8,128)S(1)} fusion(s32[3072]{0:T(1024)S(1)} %copy-done.6, bf16[3072,33]{0,1:T(8,128)(2,1)S(1)} %get-tuple-element.13, bf16[3072,33]{0,1:T(8,128)(2,1)S(1)} %get-tuple-element.14, bf16[3072,33]{0,1:T(8,128)(2,1)S(1)} %get-tuple-element.12), kind=kOutput, calls=%fused_computation.1 | convolution fusion | flops 1879824384 | bytes 1837056 | tf_op jit(solution)/shard_map/dot_general | solution.py:78
  103.6 0.9 slice_add_fusion
  104.5 2.7 copy.35
  107.1 3.8 %all_to_all.17 = f32[16,1,6336]{2,1,0:T(1,128)} reshape(f32[3072,33]{1,0:T(8,128)} %copy.35) | data formatting | bytes 811008 | tf_op jit(solution)/shard_map/all_to_all | solution.py:80
  111.0 25.5 %all_to_all.20 = f32[16,1,6336]{2,1,0:T(1,128)} all-to-all(f32[16,1,6336]{2,1,0:T(1,128)} %all_to_all.17), channel_id=1, replica_groups=mesh['gene'=8,'bin'=16] {'bin'}, dimensions={0} | all-to-all | bytes 811008 | tf_op jit(solution)/shard_map/all_to_all | solution.py:80
  136.4 2.7 reduce.2
  139.2 4.0 %reshape.98 = f32[3072,33]{1,0:T(8,128)} reshape(f32[16,6336]{1,0:T(8,128)} %reduce.2) | data formatting | bytes 811008 | tf_op jit(solution)/shard_map/reshape | solution.py:82
  143.1 2.6 copy.47
  145.7 2.3 fusion.6
  148.1 4.8 %fusion.5 = f32[3072,32]{0,1:T(8,128)} fusion(f32[3072,256]{1,0:T(8,128)S(1)} %copy-done, f32[3072,32]{0,1:T(8,128)S(1)} %copy.43, f32[3328,32]{0,1:T(8,128)} %bitcast.57, f32[3072,32]{0,1:T(8,128)} %copy.47, f32[3072]{0:T(1024)S(1)} %fusion.6), kind=kOutput, calls=%fused_computation.7 | convolution fusion | flops 302579712 | bytes 4763648 | tf_op jit(solution)/shard_map/dot_general | solution.py:107
  153.0 68.1 %all-gather.3.cloned.1.call-done = f32[3072,256]{0,1:T(8,128)} async-done(((f32[3072,32]{0,1:T(8,128)}), f32[3072,256]{0,1:T(8,128)}) %all-gather.3.cloned.1.call-update) | async-done | bytes 3145744 | tf_op jit(solution)/shard_map/all_gather | solution.py:111
  221.1 10.3 %fusion.11 = f32[256,2304]{1,0:T(8,128)S(1)} fusion(bf16[3072,2304]{1,0:T(8,128)(2,1)} %param.5, f32[3072,256]{0,1:T(8,128)} %all-gather.3.cloned.1.call-done), kind=kOutput, calls=%fused_computation.18 | convolution fusion | flops 3624665088 | bytes 19660800 | tf_op jit(solution)/shard_map/dot_general | solution.py:114
  232.1 1.8 pad_maximum_fusion.1
  234.0 71.9 %reduce-scatter.5.cloned.1.call-done = f32[16,2560]{1,0:T(8,128)} async-done(((f32[256,2560]{1,0:T(8,128)}), f32[16,2560]{1,0:T(8,128)}) %reduce-scatter.5.cloned.1.call-update) | async-done | bytes 163856 | tf_op jit(solution)/shard_map/reduce_scatter | solution.py:116
  305.9 3.5 convolution_divide_fusion
  309.5 3.5 copy.39
  313.0 45.8 %all-gather.5.cloned.1.call-done = f32[256,2304]{1,0:T(8,128)} async-done(((f32[16,2304]{1,0:T(8,128)}), f32[256,2304]{1,0:T(8,128)}) %all-gather.5.cloned.1.call-update) | async-done | bytes 2359312 | tf_op jit(solution)/shard_map/all_gather | solution.py:122
  358.8 3.2 copy.57
  (43 shorter events, 4.8 us)
Async XLA Ops:
  7.2 1.9 copy-start
  9.1 3.5 copy-start.7
  19.9 38.4 %all-to-all-start = ((f32[16,1,6336]{2,1,0:T(1,128)}), f32[16,1,6336]{2,1,0:T(1,128)}, u32[]{:S(2)}, u32[]{:S(2)}) async-start(f32[16,1,6336]{2,1,0:T(1,128)} %all_to_all.16), calls=%async_computation | async-start | bytes 819200 | tf_op jit(solution)/shard_map/all_to_all | solution.py:52
  29.2 118.9 %reduce-scatter.7.cloned.1.call-start = ((), (), s32[]{:S(2)}) async-start(), calls=%async_computation.7 | async-start | bytes 3833856
  29.2 11.5 %copy-start.2 = (f32[256,2304]{1,0:T(8,128)S(1)}, f32[256,2304]{1,0:T(8,128)}, u32[]{:S(2)}) copy-start(f32[256,2304]{1,0:T(8,128)} %param.7) | copy-start | bytes 7077892
  30.1 7.7 %copy-start.3 = (f32[12,256]{1,0:T(8,128)}, f32[12,256]{1,0:T(8,128)S(1)}, u32[]{:S(2)}) copy-start(f32[12,256]{1,0:T(8,128)S(1)} %get-tuple-element.25) | copy-start | bytes 36868
  30.7 26.1 %collective-permute-start.2 = (f32[256]{0:T(256)}, f32[256]{0:T(256)}, u32[]{:S(2)}, u32[]{:S(2)}) collective-permute-start(f32[256]{0:T(256)} %bitcast.4), channel_id=1, source_target_pairs={{1,0},{2,1},{3,2},{4,3},{5,4},{6,5},{7,6},{8,7},{9,8},{10,9},{11,1... | collective-permute-start | bytes 3080 | tf_op jit(solution)/shard_map/ppermute | solution.py:13
  32.7 24.0 %collective-permute-start.3 = (f32[256]{0:T(256)}, f32[256]{0:T(256)}, u32[]{:S(2)}, u32[]{:S(2)}) collective-permute-start(f32[256]{0:T(256)} %bitcast.6), channel_id=1, source_target_pairs={{0,1},{1,2},{2,3},{3,4},{4,5},{5,6},{6,7},{7,8},{8,9},{9,10},{10,1... | collective-permute-start | bytes 3080 | tf_op jit(solution)/shard_map/ppermute | solution.py:13
  55.0 166.1 %all-gather.3.cloned.1.call-start = ((), (), s32[]{:S(2)}) async-start(), calls=%async_computation.4 | async-start | bytes 3538944 | tf_op jit(solution)/shard_map/all_gather | solution.py:111
  70.1 8.6 %copy-start.5 = (s32[3072]{0:T(1024)}, s32[3072]{0:T(1024)S(1)}, u32[]{:S(2)}) copy-start(s32[3072]{0:T(1024)S(1)} %fusion.8) | copy-start | bytes 36868
  78.8 2.7 copy-start.4
  82.6 7.6 %collective-permute-start = (f32[256,32]{0,1:T(8,128)S(1)}, f32[256,32]{0,1:T(8,128)S(1)}, u32[]{:S(2)}, u32[]{:S(2)}) collective-permute-start(f32[256,32]{0,1:T(8,128)S(1)} %bitcast.55), channel_id=1, source_target_pairs={{1,0},{2,1},{3,2},{4,3},{5,4},{6,5},{7,6},{8,7},{9,8},{10,9},{11,1... | collective-permute-start | bytes 98312 | tf_op jit(solution)/shard_map/ppermute | solution.py:13
  84.6 6.9 %collective-permute-start.1 = (f32[256,32]{0,1:T(8,128)S(1)}, f32[256,32]{0,1:T(8,128)S(1)}, u32[]{:S(2)}, u32[]{:S(2)}) collective-permute-start(f32[256,32]{0,1:T(8,128)S(1)} %bitcast.56), channel_id=1, source_target_pairs={{0,1},{1,2},{2,3},{3,4},{4,5},{5,6},{6,7},{7,8},{8,9},{9,10},{10,1... | collective-permute-start | bytes 98312 | tf_op jit(solution)/shard_map/ppermute | solution.py:13
  91.8 3.8 %copy-start.6 = (s32[3072]{0:T(1024)S(1)}, s32[3072]{0:T(1024)}, u32[]{:S(2)}) copy-start(s32[3072]{0:T(1024)} %copy-done.5) | copy-start | bytes 36868
  152.9 153.0 %reduce-scatter.5.cloned.1.call-start = ((), (), s32[]{:S(2)}) async-start(), calls=%async_computation.5 | async-start | bytes 2785280 | tf_op jit(solution)/shard_map/reduce_scatter | solution.py:116
  221.1 10.3 %copy-start.1 = (f32[3072,256]{0,1:T(8,128)S(1)}, f32[3072,256]{0,1:T(8,128)}, u32[]{:S(2)}) copy-start(f32[3072,256]{0,1:T(8,128)} %all-gather.3.cloned.1.call-done) | copy-start | bytes 9437188
  233.9 124.9 %all-gather.5.cloned.1.call-start = ((), (), s32[]{:S(2)}) async-start(), calls=%async_computation.6 | async-start | bytes 2506752 | tf_op jit(solution)/shard_map/all_gather | solution.py:122
Sparse Core Ops, SparseCore 0:
  55.1 83.0 reduce-scatter.6
  153.0 68.0 all-gather.2
  234.0 71.8 reduce-scatter.4
  309.6 49.1 all-gather.4
where the time goes:
time: 375 us; the launch traced here: 369 us
  waiting for transfers between devices  187 us (50%)
  local copies, waits for them, and re-layouts  50.9 us (14%)
  matrix products  45 us (12%)
  blocking collectives  25.5 us (7%)
  starting transfers between devices  24.2 us (6%)
  other arithmetic  21.8 us (6%)
  between operations  14.3 us (4%)
    reduce_scatter x1, waiting for transfers between devices, on_device(): lax.psum_scatter(jnp.concatenate([cross_part, fgram_part], 1), 'bin', sca...  71.9 us
    all_gather x1, waiting for transfers between devices, on_device(): factors_new = lax.all_gather(new_own, 'gene', axis=1, tiled=True)  68.1 us
    all_gather x1, waiting for transfers between devices, on_device(): loadings_new = lax.all_gather(new_load, 'bin', axis=0, tiled=True)  45.8 us
    all_to_all x1, blocking collectives, stencil_term(): lax.all_to_all(back_rows.reshape(bin_count, group_size * (width + 1)), 'b...  25.5 us
    unnamed x27, local copies, waits for them, and re-layouts  22.6 us
    ppermute x4, starting transfers between devices, passed_along(): return lax.ppermute(block, axis, route)  14.3 us
    dot_general x1, matrix products, on_device(): lax.dot_general(fac_bf, counts, left_dims, preferred_element_type=jnp.flo...  10.3 us
    all_to_all x1, starting transfers between devices, stencil_term(): lax.all_to_all(payload.reshape(bin_count, group_size * (width + 1)), 'bin...  9.29 us
  transfers between devices with their start and end apart: 9, of which 4 were waited for; matrix products, arithmetic and copies ran while one was open for 21% of the time, Pallas kernels for 0%

commit v1 on v0

--- a/solution.py
+++ b/solution.py
@@ -108,7 +108,9 @@
         + penalty * degree[:, None] * own
     )
     new_own = own * (numer + penalty * smooth) / denom
-    factors_new = lax.all_gather(new_own, "gene", axis=1, tiled=True)
+    factors_new = jnp.concatenate(
+        lax.all_to_all(jnp.stack([new_own] * lax.axis_size("gene")), "gene", 0, 0), axis=1
+    )
     fac_bf = factors_new.astype(jnp.bfloat16)
     left_dims = (((0,), (0,)), ((), ()))
     cross_part = lax.dot_general(fac_bf, counts, left_dims, preferred_element_type=jnp.float32)

time: 375 us -> 343 us (0.915)
  waiting for transfers between devices: 187 us -> 116 us
  blocking collectives: 25.5 us -> 67.1 us
    all_gather x1 -> x0, waiting for transfers between devices: 68.1 us -> none  [on_device(): factors_new = lax.all_gather(new_own, 'gene', axis=1, tiled=True)]
    all_to_all x0 -> x1, blocking collectives: none -> 41.6 us  [on_device(): lax.all_to_all(jnp.stack([new_own] * lax.axis_size('gene')), 'gene', 0, 0)]
  transfers between devices with their start and end apart: 9 -> 8, of which waited for: 4 -> 3; matrix products, arithmetic and copies ran while one was open for 21% -> 23% of each run, Pallas kernels for 0% -> 0%
where the time goes in v1:
time: 343 us; the launch traced here: 337 us
  waiting for transfers between devices  116 us (34%)
  blocking collectives  67.1 us (20%)
  local copies, waits for them, and re-layouts  51.3 us (15%)
  matrix products  42.6 us (12%)
  starting transfers between devices  24.2 us (7%)
  other arithmetic  22 us (6%)
  between operations  14.3 us (4%)
    reduce_scatter x1, waiting for transfers between devices, on_device(): lax.psum_scatter(jnp.concatenate([cross_part, fgram_part], 1), 'bin', sca...  68.7 us
    all_gather x1, waiting for transfers between devices, on_device(): loadings_new = lax.all_gather(new_load, 'bin', axis=0, tiled=True)  45.8 us
    all_to_all x1, blocking collectives, on_device(): lax.all_to_all(jnp.stack([new_own] * lax.axis_size('gene')), 'gene', 0, 0)  41.6 us
    all_to_all x1, blocking collectives, stencil_term(): lax.all_to_all(back_rows.reshape(bin_count, group_size * (width + 1)), 'b...  25.5 us
    unnamed x27, local copies, waits for them, and re-layouts  22.6 us
    ppermute x4, starting transfers between devices, passed_along(): return lax.ppermute(block, axis, route)  14.3 us
    all_to_all x1, starting transfers between devices, stencil_term(): lax.all_to_all(payload.reshape(bin_count, group_size * (width + 1)), 'bin...  9.29 us
    dot_general x1, matrix products, on_device(): lax.dot_general(fac_bf, counts, left_dims, preferred_element_type=jnp.flo...  8.71 us
  transfers between devices with their start and end apart: 8, of which 3 were waited for; matrix products, arithmetic and copies ran while one was open for 23% of the time, Pallas kernels for 0%

profile of v1, /device:TPU:1, one launch (start us, length us, event | category | flops | bytes accessed | tf_op | source)
XLA Modules:
  0.0 337.2 jit_solution(11375970078732196236)
XLA Ops:
  7.2 1.9 copy-done
  9.1 1.6 constant_dynamic-slice_fusion
  10.7 1.8 copy.45
  12.5 0.8 pad_maximum_fusion.2
  13.4 2.7 copy.32
  16.0 3.8 %all_to_all.20 = f32[16,1,6336]{2,1,0:T(1,128)} reshape(f32[3072,33]{1,0:T(8,128)} %copy.32) | data formatting | bytes 811008 | tf_op jit(solution)/shard_map/all_to_all | solution.py:52
  19.9 9.3 %all-to-all-start = ((f32[16,1,6336]{2,1,0:T(1,128)}), f32[16,1,6336]{2,1,0:T(1,128)}, u32[]{:S(2)}, u32[]{:S(2)}) async-start(f32[16,1,6336]{2,1,0:T(1,128)} %all_to_all.20), calls=%async_computation | async-start | bytes 819200 | tf_op jit(solution)/shard_map/all_to_all | solution.py:52
  29.2 0.9 fusion.40
  30.7 2.0 collective-permute-start.2
  32.7 5.0 %collective-permute-start.3 = (f32[256]{0:T(256)}, f32[256]{0:T(256)}, u32[]{:S(2)}, u32[]{:S(2)}) collective-permute-start(f32[256]{0:T(256)} %bitcast.6), channel_id=1, source_target_pairs={{0,1},{1,2},{2,3},{3,4},{4,5},{5,6},{6,7},{7,8},{8,9},{9,10},{10,1... | collective-permute-start | bytes 3080 | tf_op jit(solution)/shard_map/ppermute | solution.py:13
  37.8 2.9 fusion.21
  40.7 7.2 %fusion.23 = f32[3072,256]{1,0:T(8,128)S(1)} fusion(bf16[3072,2304]{1,0:T(8,128)(2,1)} %param.5, f32[256,2304]{1,0:T(8,128)S(1)} %copy-done.2), kind=kOutput, calls=%fused_computation.35 | convolution fusion | flops 3624468480 | bytes 19660800 | tf_op jit(solution)/shard_map/dot_general | solution.py:97
  47.9 2.0 pad_maximum_fusion
  49.9 5.0 %copy.43 = f32[3328,256]{0,1:T(8,128)} copy(f32[3328,256]{1,0:T(8,128)} %pad_maximum_fusion) | data formatting | bytes 6815744
  56.8 0.9 fusion.37
  58.3 2.7 reduce
  61.0 4.0 %reshape.104 = f32[3072,33]{1,0:T(8,128)} reshape(f32[16,6336]{1,0:T(8,128)} %reduce) | data formatting | bytes 811008 | tf_op jit(solution)/shard_map/reshape | solution.py:54
  65.0 2.9 copy.46
  67.8 2.3 fusion.8
  70.1 1.1 reduce-precision_convert_fusion.3
  71.2 7.5 %fusion.1 = f32[3072,96]{0,1:T(8,128)S(1)} fusion(s32[3072]{0:T(1024)S(1)} %fusion.8, bf16[3072,32]{0,1:T(8,128)(2,1)S(1)} %get-tuple-element.18, bf16[3072,32]{0,1:T(8,128)(2,1)S(1)} %get-tuple-element.19, bf16[3072,32]{0,1:T(8,128)(2,1)S(1)} %get-tuple-element.17), kind=kOutput, calls=%fused_computation.2 | convolution fusion | flops 1823145984 | bytes 1781760 | tf_op jit(solution)/shard_map/dot_general | solution.py:58
  78.8 0.8 slice_add_fusion.2
  79.6 1.9 reshape.105
  81.5 1.1 broadcast_multiply_fusion
  82.6 1.9 collective-permute-start
  84.6 5.3 %collective-permute-start.1 = (f32[256,32]{0,1:T(8,128)S(1)}, f32[256,32]{0,1:T(8,128)S(1)}, u32[]{:S(2)}, u32[]{:S(2)}) collective-permute-start(f32[256,32]{0,1:T(8,128)S(1)} %bitcast.66), channel_id=1, source_target_pairs={{0,1},{1,2},{2,3},{3,4},{4,5},{5,6},{6,7},{7,8},{8,9},{9,10},{10,1... | collective-permute-start | bytes 98312 | tf_op jit(solution)/shard_map/ppermute | solution.py:13
  90.3 1.2 collective-permute-done.1
  92.0 0.8 constant_dynamic-update-slice_fusion
  92.8 1.6 dynamic-update-slice.1
  94.4 1.1 reduce-precision_convert_fusion.1
  95.5 8.0 %fusion = f32[3072,99]{0,1:T(8,128)S(1)} fusion(s32[3072]{0:T(1024)S(1)} %copy-done.6, bf16[3072,33]{0,1:T(8,128)(2,1)S(1)} %get-tuple-element.15, bf16[3072,33]{0,1:T(8,128)(2,1)S(1)} %get-tuple-element.16, bf16[3072,33]{0,1:T(8,128)(2,1)S(1)} %get-tuple-element.14), kind=kOutput, calls=%fused_computation.1 | convolution fusion | flops 1879824384 | bytes 1837056 | tf_op jit(solution)/shard_map/dot_general | solution.py:78
  103.6 0.9 slice_add_fusion
  104.5 2.7 copy.37
  107.1 3.8 %all_to_all.21 = f32[16,1,6336]{2,1,0:T(1,128)} reshape(f32[3072,33]{1,0:T(8,128)} %copy.37) | data formatting | bytes 811008 | tf_op jit(solution)/shard_map/all_to_all | solution.py:80
  111.0 25.5 %all_to_all.25 = f32[16,1,6336]{2,1,0:T(1,128)} all-to-all(f32[16,1,6336]{2,1,0:T(1,128)} %all_to_all.21), channel_id=1, replica_groups=mesh['gene'=8,'bin'=16] {'bin'}, dimensions={0} | all-to-all | bytes 811008 | tf_op jit(solution)/shard_map/all_to_all | solution.py:80
  136.5 2.7 reduce.2
  139.2 4.0 %reshape.108 = f32[3072,33]{1,0:T(8,128)} reshape(f32[16,6336]{1,0:T(8,128)} %reduce.2) | data formatting | bytes 811008 | tf_op jit(solution)/shard_map/reshape | solution.py:82
  143.2 2.6 copy.49
  145.8 2.3 fusion.6
  148.1 4.1 %fusion.5 = f32[3072,32]{0,1:T(8,128)S(1)} fusion(f32[3072,256]{1,0:T(8,128)S(1)} %copy-done, f32[3072,32]{0,1:T(8,128)S(1)} %copy.45, f32[3328,32]{0,1:T(8,128)} %bitcast.67, f32[3072,32]{0,1:T(8,128)} %copy.49, f32[3072]{0:T(1024)S(1)} %fusion.6), kind=kOutput, calls=%fused_computation.7 | convolution fusion | flops 302579712 | bytes 4763648 | tf_op jit(solution)/shard_map/dot_general | solution.py:107
  152.5 41.6 %all_to_all.26 = f32[8,3072,32]{1,2,0:T(8,128)S(1)} all-to-all(f32[8,3072,32]{1,2,0:T(8,128)S(1)} %stack.2), channel_id=1, replica_groups=mesh['gene'=8,'bin'=16] {'gene'}, dimensions={0} | all-to-all | bytes 6291456 | tf_op jit(solution)/shard_map/all_to_all | solution.py:112
  194.1 8.7 %fusion.9 = f32[256,2304]{1,0:T(8,128)S(1)} fusion(bf16[3072,2304]{1,0:T(8,128)(2,1)} %param.5, f32[3072,256]{0,1:T(8,128)S(1)} %bitcast.55), kind=kOutput, calls=%fused_computation.17 | convolution fusion | flops 3624665088 | bytes 19660800 | tf_op jit(solution)/shard_map/dot_general | solution.py:116
  203.7 1.8 pad_maximum_fusion.1
  205.6 68.7 %reduce-scatter.5.cloned.1.call-done = f32[16,2560]{1,0:T(8,128)} async-done(((f32[256,2560]{1,0:T(8,128)}), f32[16,2560]{1,0:T(8,128)}) %reduce-scatter.5.cloned.1.call-update) | async-done | bytes 163856 | tf_op jit(solution)/shard_map/reduce_scatter | solution.py:118
  274.3 3.5 %convolution_divide_fusion = f32[16,2304]{1,0:T(8,128)} fusion(f32[256,2304]{1,0:T(8,128)} %param.7, f32[16,2560]{1,0:T(8,128)} %reduce-scatter.5.cloned.1.call-done, s32[]{:T(128)S(6)} %select_n.7), kind=kOutput, calls=%fused_computation.9 | convolution fusion | flops 113319936 | bytes 2818052 | tf_op jit(solution)/shard_map/dot_general | solution.py:123
  277.9 3.5 %copy.41 = f32[3072,256]{1,0:T(8,128)} copy(f32[3072,256]{0,1:T(8,128)} %bitcast.56) | data formatting | bytes 6291456
  281.4 45.8 %all-gather.2.cloned.1.call-done = f32[256,2304]{1,0:T(8,128)} async-done(((f32[16,2304]{1,0:T(8,128)}), f32[256,2304]{1,0:T(8,128)}) %all-gather.2.cloned.1.call-update) | async-done | bytes 2359312 | tf_op jit(solution)/shard_map/all_gather | solution.py:124
  327.2 3.2 copy.59
  (43 shorter events, 5.3 us)
Async XLA Ops:
  7.2 1.9 copy-start
  9.1 3.5 %copy-start.7 = (s32[3072]{0:T(1024)S(1)}, s32[3072]{0:T(1024)}, u32[]{:S(2)}) copy-start(s32[3072]{0:T(1024)} %param.8) | copy-start | bytes 36868
  19.9 38.4 %all-to-all-start = ((f32[16,1,6336]{2,1,0:T(1,128)}), f32[16,1,6336]{2,1,0:T(1,128)}, u32[]{:S(2)}, u32[]{:S(2)}) async-start(f32[16,1,6336]{2,1,0:T(1,128)} %all_to_all.20), calls=%async_computation | async-start | bytes 819200 | tf_op jit(solution)/shard_map/all_to_all | solution.py:52
  29.2 118.9 %reduce-scatter.7.cloned.1.call-start = ((), (), s32[]{:S(2)}) async-start(), calls=%async_computation.7 | async-start | bytes 3833856
  29.2 11.5 %copy-start.2 = (f32[256,2304]{1,0:T(8,128)S(1)}, f32[256,2304]{1,0:T(8,128)}, u32[]{:S(2)}) copy-start(f32[256,2304]{1,0:T(8,128)} %param.7) | copy-start | bytes 7077892
  30.1 7.7 %copy-start.3 = (f32[12,256]{1,0:T(8,128)}, f32[12,256]{1,0:T(8,128)S(1)}, u32[]{:S(2)}) copy-start(f32[12,256]{1,0:T(8,128)S(1)} %get-tuple-element.27) | copy-start | bytes 36868
  30.7 26.1 %collective-permute-start.2 = (f32[256]{0:T(256)}, f32[256]{0:T(256)}, u32[]{:S(2)}, u32[]{:S(2)}) collective-permute-start(f32[256]{0:T(256)} %bitcast.4), channel_id=1, source_target_pairs={{1,0},{2,1},{3,2},{4,3},{5,4},{6,5},{7,6},{8,7},{9,8},{10,9},{11,1... | collective-permute-start | bytes 3080 | tf_op jit(solution)/shard_map/ppermute | solution.py:13
  32.7 24.0 %collective-permute-start.3 = (f32[256]{0:T(256)}, f32[256]{0:T(256)}, u32[]{:S(2)}, u32[]{:S(2)}) collective-permute-start(f32[256]{0:T(256)} %bitcast.6), channel_id=1, source_target_pairs={{0,1},{1,2},{2,3},{3,4},{4,5},{5,6},{6,7},{7,8},{8,9},{9,10},{10,1... | collective-permute-start | bytes 3080 | tf_op jit(solution)/shard_map/ppermute | solution.py:13
  55.0 219.3 %reduce-scatter.5.cloned.1.call-start = ((), (), s32[]{:S(2)}) async-start(), calls=%async_computation.5 | async-start | bytes 2785280 | tf_op jit(solution)/shard_map/reduce_scatter | solution.py:118
  70.1 8.6 %copy-start.5 = (s32[3072]{0:T(1024)}, s32[3072]{0:T(1024)S(1)}, u32[]{:S(2)}) copy-start(s32[3072]{0:T(1024)S(1)} %fusion.8) | copy-start | bytes 36868
  78.8 2.7 copy-start.4
  82.6 7.6 %collective-permute-start = (f32[256,32]{0,1:T(8,128)S(1)}, f32[256,32]{0,1:T(8,128)S(1)}, u32[]{:S(2)}, u32[]{:S(2)}) collective-permute-start(f32[256,32]{0,1:T(8,128)S(1)} %bitcast.65), channel_id=1, source_target_pairs={{1,0},{2,1},{3,2},{4,3},{5,4},{6,5},{7,6},{8,7},{9,8},{10,9},{11,1... | collective-permute-start | bytes 98312 | tf_op jit(solution)/shard_map/ppermute | solution.py:13
  84.6 6.9 %collective-permute-start.1 = (f32[256,32]{0,1:T(8,128)S(1)}, f32[256,32]{0,1:T(8,128)S(1)}, u32[]{:S(2)}, u32[]{:S(2)}) collective-permute-start(f32[256,32]{0,1:T(8,128)S(1)} %bitcast.66), channel_id=1, source_target_pairs={{0,1},{1,2},{2,3},{3,4},{4,5},{5,6},{6,7},{7,8},{8,9},{9,10},{10,1... | collective-permute-start | bytes 98312 | tf_op jit(solution)/shard_map/ppermute | solution.py:13
  91.8 3.8 %copy-start.6 = (s32[3072]{0:T(1024)S(1)}, s32[3072]{0:T(1024)}, u32[]{:S(2)}) copy-start(s32[3072]{0:T(1024)} %copy-done.5) | copy-start | bytes 36868
  194.1 8.7 %copy-start.1 = (f32[8,3072,32]{1,2,0:T(8,128)}, f32[8,3072,32]{1,2,0:T(8,128)S(1)}, u32[]{:S(2)}) copy-start(f32[8,3072,32]{1,2,0:T(8,128)S(1)} %all_to_all.26) | copy-start | bytes 9437188
  205.6 121.7 %all-gather.2.cloned.1.call-start = ((), (), s32[]{:S(2)}) async-start(), calls=%async_computation.6 | async-start | bytes 2506752 | tf_op jit(solution)/shard_map/all_gather | solution.py:124
Sparse Core Ops, SparseCore 0:
  55.1 83.0 reduce-scatter.6
  205.7 68.5 reduce-scatter.4
  278.0 49.2 all-gather.1
